TPU v7x, 32 devices: a whole 2x2x4 slice. The times are simulated.
32 devices in a mesh: ctx: 8 (over z, x), tp: 4 (over y, core).
Axes of the slice: x: 2, y: 2, z: 4, core: 2. Of those that a mesh axis runs over, the one named last changes fastest.
Arguments:
- tokens: bfloat16 [4096, 4096], P(('ctx', 'tp')), may hold values from -6 to 6
- in_weight: bfloat16 [4096, 3, 4096], P('ctx', None, 'tp'), may hold values from -0.09375 to 0.09375
- short_filter: float32 [3, 3, 4096], P(None, None, 'tp'), may hold values from -3 to 3
- decay_rates: float32 [16, 4096], P(None, 'tp'), may hold values from 1.2207031e-05 to 0.1, as said below
- residues: float32 [16, 4096], P(None, 'tp'), may hold values from -1.5 to 1.5
- skip_gain: float32 [4096], P('tp'), may hold values from -4 to 4
Outputs:
- mixed: bfloat16 [4096, 4096], P('ctx', 'tp')
Inputs may be any that keep to these rules, and one draw needn't show every extreme that they name: `decay_rates`: positive decay rates.
All inputs are finite; a program needn't handle non-finite values.
Results may differ from a plain program's by a relative error of at most 0.0063.
Values may be sent and summed in bfloat16 or wider, within the bound.
A program may use at most 128 MiB of HBM per device.

v0:
```python
import jax
import jax.numpy as jnp
from jax import lax
from jax.sharding import PartitionSpec as P

BLOCK = 32


def passed_along(value, axis, steps):
    count = lax.axis_size(axis)
    initial, last = (max(0, -steps), min(count, count - steps))
    return lax.ppermute(value, axis, [(source, source + steps) for source in range(initial, last)])


def block_scan(product, decay_rates, residues, block):
    channels = product.shape[1]
    mode_gain = residues * jnp.sqrt(2.0 * decay_rates)
    positions = jnp.arange(block, dtype=jnp.float32)
    kernel = jnp.sum(
        mode_gain[None] * jnp.exp(-decay_rates[None] * positions[:, None, None]), axis=1
    )
    gaps = jnp.arange(block, dtype=jnp.int32)[:, None] - jnp.arange(block, dtype=jnp.int32)[None, :]
    toeplitz = jnp.where(
        (gaps >= 0)[:, :, None], kernel[jnp.clip(gaps, 0, block - 1)], jnp.float32(0.0)
    )
    read_out = mode_gain[None] * jnp.exp(-decay_rates[None] * (positions[:, None, None] + 1.0))
    take_in = jnp.exp(-decay_rates[None] * (block - 1.0 - positions)[:, None, None])
    step_decay = jnp.exp(-decay_rates * block)

    def advance(state, block_in):
        block_out = jnp.sum(toeplitz * block_in[None], axis=1) + jnp.sum(
            read_out * state[None], axis=1
        )
        state = step_decay * state + jnp.sum(take_in * block_in[:, None, :], axis=0)
        return (state, block_out)

    zero_state = jnp.zeros(decay_rates.shape, jnp.float32)
    state, outputs = lax.scan(advance, zero_state, product.reshape(-1, block, channels))
    return (outputs.reshape(-1, channels), state)


def per_device(tokens, in_weight, short_filter, decay_rates, residues, skip_gain):
    gathered = lax.all_gather(tokens, "tp", axis=0, tiled=True)
    length = gathered.shape[0]
    channels = in_weight.shape[2]
    short_lag = short_filter.shape[1] - 1
    flat_weight = in_weight.reshape(in_weight.shape[0], 3 * channels)
    projected = jnp.dot(
        gathered,
        lax.all_gather(flat_weight, "ctx", axis=0, tiled=True),
        preferred_element_type=jnp.float32,
    ).astype(jnp.bfloat16)
    prior_rows = passed_along(projected[length - short_lag :], "ctx", 1)
    padded = jnp.concatenate([prior_rows, projected], axis=0)
    widened = padded.astype(jnp.float32).reshape(length + short_lag, 3, channels)
    features = jnp.zeros((length, 3, channels), jnp.float32)
    for offset in range(short_lag + 1):
        features = (
            features
            + short_filter[None, :, offset, :]
            * widened[short_lag - offset : short_lag - offset + length]
        )
    product = features[:, 1] * features[:, 2]
    inside, outgoing = block_scan(product, decay_rates, residues, BLOCK)
    every_state = lax.all_gather(outgoing[None], "ctx", axis=0, tiled=True)
    shard_count = every_state.shape[0]
    own_index = lax.axis_index("ctx")
    sources = jnp.arange(shard_count, dtype=jnp.int32)
    distance = own_index - 1 - sources
    earlier = distance >= 0
    steps_back = jnp.where(earlier, distance, 0).astype(jnp.float32)
    factors = jnp.exp(-decay_rates[None] * (length * steps_back)[:, None, None])
    factors = jnp.where(earlier[:, None, None], factors, jnp.float32(0.0))
    incoming = jnp.sum(factors * every_state, axis=0)
    mode_gain = residues * jnp.sqrt(2.0 * decay_rates)
    offsets = jnp.arange(1, length + 1, dtype=jnp.float32)
    carried = jnp.sum(
        mode_gain[None] * jnp.exp(-decay_rates[None] * offsets[:, None, None]) * incoming[None],
        axis=1,
    )
    longconv = inside + carried
    return (features[:, 0] * (longconv + skip_gain[None] * product)).astype(jnp.bfloat16)


def solution(mesh):
    in_specs = (
        P(("ctx", "tp"), None),
        P("ctx", None, "tp"),
        P(None, None, "tp"),
        P(None, "tp"),
        P(None, "tp"),
        P("tp"),
    )
    out_specs = P("ctx", "tp")
    return jax.shard_map(
        per_device, mesh=mesh, in_specs=in_specs, out_specs=out_specs, check_vma=False
    )
```

profile of v0, /device:TPU:0, one launch (start us, length us, event | category | flops | bytes accessed | tf_op | source)
XLA Modules:
  0.0 757.3 jit_solution(17259507543595357559)
XLA Ops:
  7.3 4.6 copy.24
  12.7 5.4 gather_fusion
  18.2 4.9 broadcast_select_fusion.1
  23.2 22.9 %all-gather.4.cloned.1.call-done = bf16[512,4096]{1,0:T(8,128)(2,1)} async-done(((bf16[128,4096]{1,0:T(8,128)(2,1)}), bf16[512,4096]{1,0:T(8,128)(2,1)}) %all-gather.4.cloned.1.call-update) | async-done | bytes 4194320 | tf_op jit(solution)/shard_map/all_gather | solution.py:43
  46.1 481.9 %all-gather.6.cloned.1.call-done = bf16[4096,3072]{0,1:T(8,128)(2,1)} async-done(((bf16[512,3072]{0,1:T(8,128)(2,1)}), bf16[4096,3072]{0,1:T(8,128)(2,1)}) %all-gather.6.cloned.1.call-update) | async-done | bytes 25165840 | tf_op jit(solution)/shard_map/all_gather | solution.py:50
  528.0 18.2 %convolution_convert_fusion = bf16[512,3072]{1,0:T(8,128)(2,1)S(1)} fusion(bf16[512,4096]{1,0:T(8,128)(2,1)} %all-gather.4.cloned.1.call-done, bf16[4096,3072]{0,1:T(8,128)(2,1)} %all-gather.6.cloned.1.call-done), kind=kOutput, calls=%fused_computation.14 | convolution fusion | flops 12886474752 | bytes 32505856 | tf_op jit(solution)/shard_map/dot_general | solution.py:48
  552.8 6.6 fusion.10
  559.4 6.6 copy.29
  566.0 6.6 copy.30
  572.5 6.6 copy.27
  579.1 6.6 copy.28
  585.7 6.6 copy.25
  592.3 6.5 copy.26
  598.8 8.8 %multiply_add_fusion.1 = f32[512,3,1024]{2,0,1:T(8,128)S(1)} fusion(f32[512,3,1024]{2,0,1:T(8,128)} %copy.30, f32[512,3,1024]{2,0,1:T(8,128)} %copy.28, f32[512,3,1024]{2,0,1:T(8,128)} %copy.26, f32[3,1024]{1,0:T(4,128)S(1)} %get-tuple-element.187, f32[3,1024]{1,0:T(4,128)S(1)} %get-tuple-element.188, f32[3,1024]{1,0:T(4,128)S(1)} %bitcast.51), kind=kLoop, calls=%fused_computation.13 | loop fusion | flops 7864320 | bytes 25202688 | tf_op jit(solution)/shard_map/add | solution.py:59
  612.0 90.5 %while.15 = (s32[]{:T(128)}, f32[16,1024]{1,0:T(8,128)S(1)}, f32[16,32,1024]{2,1,0:T(8,128)}, f32[16,1024]{1,0:T(8,128)S(1)}, f32[16,32,1024]{2,1,0:T(8,128)}, /...) while((s32[]{:T(128)}, f32[16,1024]{1,0:T(8,128)S(1)}, ...), condition=%wide.region_5.6_spmd.clone.clone.clone, body=%wide.region_1.5_spmd.clone.clone.clone.sunk | while | flops 5783555 | bytes 6029712 | solution.py:38
  614.1 2.9 multiply_reduce_fusion.5
  619.8 2.9 multiply_reduce_fusion.5
  625.4 2.9 multiply_reduce_fusion.5
  631.1 2.9 multiply_reduce_fusion.5
  636.7 2.9 multiply_reduce_fusion.5
  642.4 2.9 multiply_reduce_fusion.5
  648.1 2.9 multiply_reduce_fusion.5
  702.6 34.3 %all-gather = f32[128,1024]{1,0:T(8,128)S(1)} all-gather(f32[16,1024]{1,0:T(8,128)S(1)} %get-tuple-element.49), channel_id=2, replica_groups=mesh['ctx'=8,'tp'=4] {'ctx'}, dimensions={0}, use_global_device_ids=true | all-gather | bytes 589824 | tf_op jit(solution)/shard_map/all_gather | solution.py:65
  737.1 11.0 %multiply_reduce_fusion.1 = f32[512,1024]{1,0:T(8,128)S(1)} fusion(f32[16,1024]{1,0:T(8,128)S(1)} %multiply_reduce_fusion.3, f32[512]{0:T(512)S(1)} %iota_add_fusion, f32[16,1024]{1,0:T(8,128)S(1)} %get-tuple-element.298, f32[16,1024]{1,0:T(8,128)S(1)} %get-tuple-element.299), kind=kLoop, calls=%fused_computation.12 | loop fusion | flops 33030144 | bytes 2295808 | tf_op jit(solution)/shard_map/reduce_sum | solution.py:77
  (134 shorter events, 84.8 us)
Async XLA Ops:
  6.5 39.6 %all-gather.4.cloned.1.call-start = ((), (), s32[]{:S(2)}) async-start(), calls=%async_computation | async-start | bytes 5242880 | tf_op jit(solution)/shard_map/all_gather | solution.py:43
  7.3 4.8 copy-start.3
  7.3 4.8 copy-start.4
  7.3 520.8 %all-gather.6.cloned.1.call-start = ((), (), s32[]{:S(2)}) async-start(), calls=%async_computation.1 | async-start | bytes 28311552 | tf_op jit(solution)/shard_map/all_gather | solution.py:50
  12.7 5.5 copy-start.5
  546.2 2.5 copy-start.1
  546.3 3.7 collective-permute-start
  607.6 2.7 copy-start
  736.9 11.3 %slice-start = ((s8[6291456]{0:T(1024)(128)(4,1)}), s8[4194304]{0:T(1024)(128)(4,1)S(1)}, s32[]{:S(2)}) async-start(s8[6291456]{0:T(1024)(128)(4,1)} %bitcast.42), calls=%async_computation.2 | async-start | bytes 8388608
  737.1 11.1 %slice-start.1 = ((s8[6291456]{0:T(1024)(128)(4,1)}), s8[2097152]{0:T(1024)(128)(4,1)S(1)}, s32[]{:S(2)}) async-start(s8[6291456]{0:T(1024)(128)(4,1)} %bitcast.42), calls=%async_computation.3 | async-start | bytes 4194304
  737.1 11.1 %copy-start.2 = (f32[16,32,1024]{2,1,0:T(8,128)S(1)}, f32[16,32,1024]{2,1,0:T(8,128)}, u32[]{:S(2)}) copy-start(f32[16,32,1024]{2,1,0:T(8,128)} %get-tuple-element.48) | copy-start | bytes 6291460
  737.1 11.1 %copy-start.6 = (f32[1024]{0:T(1024)S(1)}, f32[1024]{0:T(1024)}, u32[]{:S(2)}) copy-start(f32[1024]{0:T(1024)} %param.13) | copy-start | bytes 12292
Sparse Core Ops, SparseCore 0:
  8.9 37.1 all-gather.3
  47.6 480.3 all-gather.5
where the time goes:
time: 759 us; the launch traced here: 757 us
  waiting for transfers between devices  507 us (67%)
  other arithmetic  108 us (14%)
  local copies, waits for them, and re-layouts  73.6 us (10%)
  blocking collectives  34.3 us (5%)
  matrix products  18.2 us (2%)
  between operations  13.7 us (2%)
    all_gather x1, waiting for transfers between devices, per_device(): lax.all_gather(flat_weight, 'ctx', axis=0, tiled=True)  482 us
    reduce_sum x16, other arithmetic, advance(): jnp.sum(toeplitz * block_in[None], axis=1)  46.5 us
    slice x7, local copies, waits for them, and re-layouts, per_device(): widened[short_lag - offset:short_lag - offset + length]  46 us
    all_gather x1, blocking collectives, per_device(): every_state = lax.all_gather(outgoing[None], 'ctx', axis=0, tiled=True)  34.3 us
    all_gather x1, waiting for transfers between devices, per_device(): gathered = lax.all_gather(tokens, 'tp', axis=0, tiled=True)  22.9 us
    dot_general x1, matrix products, per_device(): jnp.dot(gathered, lax.all_gather(flat_weight, 'ctx', axis=0, tiled=True),...  18.2 us
    reduce_sum x16, other arithmetic, advance(): jnp.sum(read_out * state[None], axis=1)  17.7 us
  transfers between devices with their start and end apart: 3, of which 3 were waited for; matrix products, arithmetic and copies ran while one was open for 2% of the time, Pallas kernels for 0%

commit v1 on v0

--- a/solution.py
+++ b/solution.py
@@ -4,6 +4,16 @@
 from jax.sharding import PartitionSpec as P
 
 BLOCK = 32
+
+
+def gather_around(x, axis, dim):
+    ways, here, step = (lax.axis_size(axis), lax.axis_index(axis), x.shape[dim])
+    shape = [n * ways if d == dim else n for d, n in enumerate(x.shape)]
+    full = lax.dynamic_update_slice_in_dim(jnp.zeros(shape, x.dtype), x, here * step, axis=dim)
+    for far in range(1, ways):
+        x = lax.ppermute(x, axis, [(d, (d + 1) % ways) for d in range(ways)])
+        full = lax.dynamic_update_slice_in_dim(full, x, (here - far) % ways * step, axis=dim)
+    return full
 
 
 def passed_along(value, axis, steps):
@@ -46,9 +56,7 @@
     short_lag = short_filter.shape[1] - 1
     flat_weight = in_weight.reshape(in_weight.shape[0], 3 * channels)
     projected = jnp.dot(
-        gathered,
-        lax.all_gather(flat_weight, "ctx", axis=0, tiled=True),
-        preferred_element_type=jnp.float32,
+        gathered, gather_around(flat_weight, "ctx", 0), preferred_element_type=jnp.float32
     ).astype(jnp.bfloat16)
     prior_rows = passed_along(projected[length - short_lag :], "ctx", 1)
     padded = jnp.concatenate([prior_rows, projected], axis=0)

time: 759 us -> 741 us (0.976)
  waiting for transfers between devices: 507 us -> 452 us
  local copies, waits for them, and re-layouts: 73.6 us -> 113 us
    all_gather x1 -> x0, waiting for transfers between devices: 482 us -> none  [per_device(): lax.all_gather(flat_weight, 'ctx', axis=0, tiled=True)]
    ppermute x0 -> x7, waiting for transfers between devices: none -> 451 us  [gather_around(): x = lax.ppermute(x, axis, [(d, (d + 1) % ways) for d in range(ways)])]
    all_gather x1, waiting for transfers between devices: 22.9 us -> 0.01 us  [per_device(): gathered = lax.all_gather(tokens, 'tp', axis=0, tiled=True)]
    dynamic_update_slice x0 -> x8, local copies, waits for them, and re-layouts: none -> 19.2 us  [the longest x7 17.3 us: gather_around(): lax.dynamic_update_slice_in_dim(full, x, (here - far) % ways * step, axis...]
    unnamed x21 -> x39, local copies, waits for them, and re-layouts: 7.34 us -> 18.2 us
    broadcast_in_dim x0 -> x1, local copies, waits for them, and re-layouts: none -> 9.16 us  [gather_around(): jnp.zeros(shape, x.dtype)]
  transfers between devices with their start and end apart: 3 -> 9, of which waited for: 3 -> 8; matrix products, arithmetic and copies ran while one was open for 2% -> 5% of each run, Pallas kernels for 0% -> 0%
where the time goes in v1:
time: 741 us; the launch traced here: 739 us
  waiting for transfers between devices  452 us (61%)
  local copies, waits for them, and re-layouts  113 us (15%)
  other arithmetic  106 us (14%)
  blocking collectives  31.3 us (4%)
  matrix products  18.2 us (2%)
  between operations  13.8 us (2%)
    ppermute x7, waiting for transfers between devices, gather_around(): x = lax.ppermute(x, axis, [(d, (d + 1) % ways) for d in range(ways)])  451 us
    reduce_sum x16, other arithmetic, advance(): jnp.sum(toeplitz * block_in[None], axis=1)  46.5 us
    slice x7, local copies, waits for them, and re-layouts, per_device(): widened[short_lag - offset:short_lag - offset + length]  46.1 us
    all_gather x1, blocking collectives, per_device(): every_state = lax.all_gather(outgoing[None], 'ctx', axis=0, tiled=True)  31.3 us
    dot_general x1, matrix products, per_device(): jnp.dot(gathered, gather_around(flat_weight, 'ctx', 0), preferred_element...  18.2 us
    unnamed x39, local copies, waits for them, and re-layouts  18.2 us
    reduce_sum x16, other arithmetic, advance(): jnp.sum(read_out * state[None], axis=1)  17.7 us
    dynamic_update_slice x7, local copies, waits for them, and re-layouts, gather_around(): lax.dynamic_update_slice_in_dim(full, x, (here - far) % ways * step, axis...  17.3 us
  transfers between devices with their start and end apart: 9, of which 8 were waited for; matrix products, arithmetic and copies ran while one was open for 5% of the time, Pallas kernels for 0%

profile of v1, /device:TPU:0, one launch (start us, length us, event | category | flops | bytes accessed | tf_op | source)
XLA Modules:
  0.0 739.0 jit_solution(13917274328652521850)
XLA Ops:
  6.5 3.2 copy.24
  12.8 71.1 %collective-permute-done = bf16[512,3072]{0,1:T(8,128)(2,1)S(1)} collective-permute-done((bf16[512,3072]{0,1:T(8,128)(2,1)S(1)}, bf16[512,3072]{0,1:T(8,128)(2,1)S(1)}, u32[]{:S(2)}, u32[]{:S(2)}) %collective-permute-start) | collective-permute-done | bytes 3145760 | tf_op jit(solution)/shard_map/ppermute | solution.py:14
  85.6 72.0 %collective-permute-done.1 = bf16[512,3072]{0,1:T(8,128)(2,1)S(1)} collective-permute-done((bf16[512,3072]{0,1:T(8,128)(2,1)S(1)}, bf16[512,3072]{0,1:T(8,128)(2,1)S(1)}, u32[]{:S(2)}, u32[]{:S(2)}) %collective-permute-start.1) | collective-permute-done | bytes 3145760 | tf_op jit(solution)/shard_map/ppermute | solution.py:14
  159.1 71.1 %collective-permute-done.2 = bf16[512,3072]{0,1:T(8,128)(2,1)S(1)} collective-permute-done((bf16[512,3072]{0,1:T(8,128)(2,1)S(1)}, bf16[512,3072]{0,1:T(8,128)(2,1)S(1)}, u32[]{:S(2)}, u32[]{:S(2)}) %collective-permute-start.2) | collective-permute-done | bytes 3145760 | tf_op jit(solution)/shard_map/ppermute | solution.py:14
  231.9 70.2 %collective-permute-done.3 = bf16[512,3072]{0,1:T(8,128)(2,1)S(1)} collective-permute-done((bf16[512,3072]{0,1:T(8,128)(2,1)S(1)}, bf16[512,3072]{0,1:T(8,128)(2,1)S(1)}, u32[]{:S(2)}, u32[]{:S(2)}) %collective-permute-start.3) | collective-permute-done | bytes 3145760 | tf_op jit(solution)/shard_map/ppermute | solution.py:14
  303.8 69.5 %collective-permute-done.4 = bf16[512,3072]{0,1:T(8,128)(2,1)} collective-permute-done((bf16[512,3072]{0,1:T(8,128)(2,1)S(1)}, bf16[512,3072]{0,1:T(8,128)(2,1)}, u32[]{:S(2)}, u32[]{:S(2)}) %collective-permute-start.4) | collective-permute-done | bytes 3145760 | tf_op jit(solution)/shard_map/ppermute | solution.py:14
  374.2 5.5 gather_fusion
  379.7 9.2 %broadcast_in_dim.35 = bf16[4096,3072]{0,1:T(8,128)(2,1)} broadcast(bf16[]{:T(256)} %constant.80.clone.1), dimensions={} | broadcast | bytes 25165826 | tf_op jit(solution)/shard_map/broadcast_in_dim | solution.py:12
  390.8 51.3 %collective-permute-done.5 = bf16[512,3072]{0,1:T(8,128)(2,1)} collective-permute-done((bf16[512,3072]{0,1:T(8,128)(2,1)}, bf16[512,3072]{0,1:T(8,128)(2,1)}, u32[]{:S(2)}, u32[]{:S(2)}) %collective-permute-start.5) | collective-permute-done | bytes 3145760 | tf_op jit(solution)/shard_map/ppermute | solution.py:14
  456.4 3.8 constant_dynamic-update-slice_fusion.2
  460.3 3.8 constant_dynamic-update-slice_fusion.1
  464.0 46.0 %collective-permute-done.6 = bf16[512,3072]{0,1:T(8,128)(2,1)S(1)} collective-permute-done((bf16[512,3072]{0,1:T(8,128)(2,1)}, bf16[512,3072]{0,1:T(8,128)(2,1)S(1)}, u32[]{:S(2)}, u32[]{:S(2)}) %collective-permute-start.6) | collective-permute-done | bytes 3145760 | tf_op jit(solution)/shard_map/ppermute | solution.py:14
  511.9 18.2 %fusion.6 = bf16[512,3072]{1,0:T(8,128)(2,1)S(1)} fusion(bf16[4096,3072]{0,1:T(8,128)(2,1)} %constant_dynamic-update-slice_fusion, bf16[512,4096]{1,0:T(8,128)(2,1)} %all-gather.3.cloned.1.call-done), kind=kOutput, calls=%fused_computation.15 | convolution fusion | flops 12886474752 | bytes 32505856 | tf_op jit(solution)/shard_map/dot_general | solution.py:58
  537.3 6.6 fusion.11
  543.9 6.6 copy.29
  550.5 6.6 copy.30
  557.1 6.6 copy.27
  563.7 6.6 copy.28
  570.3 6.6 copy.25
  576.8 6.5 copy.26
  583.4 8.8 %multiply_add_fusion.1 = f32[512,3,1024]{2,0,1:T(8,128)S(1)} fusion(f32[512,3,1024]{2,0,1:T(8,128)} %copy.30, f32[512,3,1024]{2,0,1:T(8,128)} %copy.28, f32[512,3,1024]{2,0,1:T(8,128)} %copy.26, f32[3,1024]{1,0:T(4,128)S(1)} %get-tuple-element.187, f32[3,1024]{1,0:T(4,128)S(1)} %get-tuple-element.188, f32[3,1024]{1,0:T(4,128)S(1)} %bitcast.54), kind=kLoop, calls=%fused_computation.13 | loop fusion | flops 7864320 | bytes 25202688 | tf_op jit(solution)/shard_map/add | solution.py:67
  596.6 90.7 %while.15 = (s32[]{:T(128)}, f32[16,1024]{1,0:T(8,128)S(1)}, f32[16,32,1024]{2,1,0:T(8,128)}, f32[16,1024]{1,0:T(8,128)S(1)}, f32[16,32,1024]{2,1,0:T(8,128)}, /...) while((s32[]{:T(128)}, f32[16,1024]{1,0:T(8,128)S(1)}, ...), condition=%wide.region_5.6_spmd.clone.clone.clone, body=%wide.region_1.5_spmd.clone.clone.clone.sunk | while | flops 5783555 | bytes 6029712 | solution.py:48
  687.3 31.3 %all-gather = f32[128,1024]{1,0:T(8,128)S(1)} all-gather(f32[16,1024]{1,0:T(8,128)S(1)} %get-tuple-element.49), channel_id=2, replica_groups=mesh['ctx'=8,'tp'=4] {'ctx'}, dimensions={0}, use_global_device_ids=true | all-gather | bytes 589824 | tf_op jit(solution)/shard_map/all_gather | solution.py:73
  718.8 11.0 %multiply_reduce_fusion.1 = f32[512,1024]{1,0:T(8,128)S(1)} fusion(f32[16,1024]{1,0:T(8,128)S(1)} %multiply_reduce_fusion.3, f32[512]{0:T(512)S(1)} %iota_add_fusion, f32[16,1024]{1,0:T(8,128)S(1)} %get-tuple-element.305, f32[16,1024]{1,0:T(8,128)S(1)} %get-tuple-element.306), kind=kLoop, calls=%fused_computation.12 | loop fusion | flops 33030144 | bytes 2295808 | tf_op jit(solution)/shard_map/reduce_sum | solution.py:85
  (172 shorter events, 132.8 us)
Async XLA Ops:
  6.5 367.0 %copy-start.12 = (f32[16,1024]{1,0:T(8,128)S(1)}, f32[16,1024]{1,0:T(8,128)}, u32[]{:S(2)}) copy-start(f32[16,1024]{1,0:T(8,128)} %param.11) | copy-start | bytes 196612
  6.5 367.0 %copy-start.13 = (f32[16,1024]{1,0:T(8,128)S(1)}, f32[16,1024]{1,0:T(8,128)}, u32[]{:S(2)}) copy-start(f32[16,1024]{1,0:T(8,128)} %param.12) | copy-start | bytes 196612
  6.5 505.4 %all-gather.3.cloned.1.call-start = ((), (), s32[]{:S(2)}) async-start(), calls=%async_computation | async-start | bytes 5242880 | tf_op jit(solution)/shard_map/all_gather | solution.py:53
  9.8 74.2 %collective-permute-start = (bf16[512,3072]{0,1:T(8,128)(2,1)S(1)}, bf16[512,3072]{0,1:T(8,128)(2,1)S(1)}, u32[]{:S(2)}, u32[]{:S(2)}) collective-permute-start(bf16[512,3072]{0,1:T(8,128)(2,1)S(1)} %bitcast.50), channel_id=1, source_target_pairs={{0,4},{4,8},{8,12},{12,16},{16,20},{20,24},{24,28},{28,0},{1,5},{5... | collective-permute-start | bytes 9437192 | tf_op jit(solution)/shard_map/ppermute | solution.py:14
  85.6 72.0 %collective-permute-start.1 = (bf16[512,3072]{0,1:T(8,128)(2,1)S(1)}, bf16[512,3072]{0,1:T(8,128)(2,1)S(1)}, u32[]{:S(2)}, u32[]{:S(2)}) collective-permute-start(bf16[512,3072]{0,1:T(8,128)(2,1)S(1)} %collective-permute-done), channel_id=1, source_target_pairs={{0,4},{4,8},{8,12},{12,16},{16,20},{20,24},{24,28},{28,0},{1,5},{5... | collective-permute-start | bytes 9437192 | tf_op jit(solution)/shard_map/ppermute | solution.py:14
  159.1 71.1 %collective-permute-start.2 = (bf16[512,3072]{0,1:T(8,128)(2,1)S(1)}, bf16[512,3072]{0,1:T(8,128)(2,1)S(1)}, u32[]{:S(2)}, u32[]{:S(2)}) collective-permute-start(bf16[512,3072]{0,1:T(8,128)(2,1)S(1)} %collective-permute-done.1), channel_id=1, source_target_pairs={{0,4},{4,8},{8,12},{12,16},{16,20},{20,24},{24,28},{28,0},{1,5},{5... | collective-permute-start | bytes 9437192 | tf_op jit(solution)/shard_map/ppermute | solution.py:14
  231.9 70.3 %collective-permute-start.3 = (bf16[512,3072]{0,1:T(8,128)(2,1)S(1)}, bf16[512,3072]{0,1:T(8,128)(2,1)S(1)}, u32[]{:S(2)}, u32[]{:S(2)}) collective-permute-start(bf16[512,3072]{0,1:T(8,128)(2,1)S(1)} %collective-permute-done.2), channel_id=1, source_target_pairs={{0,4},{4,8},{8,12},{12,16},{16,20},{20,24},{24,28},{28,0},{1,5},{5... | collective-permute-start | bytes 9437192 | tf_op jit(solution)/shard_map/ppermute | solution.py:14
  302.1 1.7 copy-start.9
  303.8 69.5 %collective-permute-start.4 = (bf16[512,3072]{0,1:T(8,128)(2,1)S(1)}, bf16[512,3072]{0,1:T(8,128)(2,1)}, u32[]{:S(2)}, u32[]{:S(2)}) collective-permute-start(bf16[512,3072]{0,1:T(8,128)(2,1)S(1)} %collective-permute-done.3), channel_id=1, source_target_pairs={{0,4},{4,8},{8,12},{12,16},{16,20},{20,24},{24,28},{28,0},{1,5},{5... | collective-permute-start | bytes 9437192 | tf_op jit(solution)/shard_map/ppermute | solution.py:14
  373.3 68.9 %collective-permute-start.5 = (bf16[512,3072]{0,1:T(8,128)(2,1)}, bf16[512,3072]{0,1:T(8,128)(2,1)}, u32[]{:S(2)}, u32[]{:S(2)}) collective-permute-start(bf16[512,3072]{0,1:T(8,128)(2,1)} %collective-permute-done.4), channel_id=1, source_target_pairs={{0,4},{4,8},{8,12},{12,16},{16,20},{20,24},{24,28},{28,0},{1,5},{5... | collective-permute-start | bytes 9437192 | tf_op jit(solution)/shard_map/ppermute | solution.py:14
  374.2 5.5 copy-start.14
  388.9 53.3 %copy-start.1 = (f32[1024,1024]{1,0:T(8,128)S(1)}, f32[1024,1024]{1,0:T(8,128)}, u32[]{:S(2)}) copy-start(f32[1024,1024]{1,0:T(8,128)} %gather_fusion) | copy-start | bytes 12582916
  442.1 67.9 %collective-permute-start.6 = (bf16[512,3072]{0,1:T(8,128)(2,1)}, bf16[512,3072]{0,1:T(8,128)(2,1)S(1)}, u32[]{:S(2)}, u32[]{:S(2)}) collective-permute-start(bf16[512,3072]{0,1:T(8,128)(2,1)} %collective-permute-done.5), channel_id=1, source_target_pairs={{0,4},{4,8},{8,12},{12,16},{16,20},{20,24},{24,28},{28,0},{1,5},{5... | collective-permute-start | bytes 9437192 | tf_op jit(solution)/shard_map/ppermute | solution.py:14
  442.2 3.3 copy-start.4
  445.4 3.0 copy-start.6
  448.5 3.0 copy-start.8
  451.5 3.0 copy-start.10
  530.1 1.7 copy-start.2
  531.8 2.7 collective-permute-start.7
  592.2 2.7 copy-start
  718.6 11.2 %slice-start = ((s8[6291456]{0:T(1024)(128)(4,1)}), s8[4194304]{0:T(1024)(128)(4,1)S(1)}, s32[]{:S(2)}) async-start(s8[6291456]{0:T(1024)(128)(4,1)} %bitcast.44), calls=%async_computation.1 | async-start | bytes 8388608
  718.8 11.0 %slice-start.1 = ((s8[6291456]{0:T(1024)(128)(4,1)}), s8[2097152]{0:T(1024)(128)(4,1)S(1)}, s32[]{:S(2)}) async-start(s8[6291456]{0:T(1024)(128)(4,1)} %bitcast.44), calls=%async_computation.2 | async-start | bytes 4194304
  718.8 11.0 %copy-start.11 = (f32[16,32,1024]{2,1,0:T(8,128)S(1)}, f32[16,32,1024]{2,1,0:T(8,128)}, u32[]{:S(2)}) copy-start(f32[16,32,1024]{2,1,0:T(8,128)} %get-tuple-element.48) | copy-start | bytes 6291460
  718.8 11.0 %copy-start.15 = (f32[1024]{0:T(1024)S(1)}, f32[1024]{0:T(1024)}, u32[]{:S(2)}) copy-start(f32[1024]{0:T(1024)} %param.13) | copy-start | bytes 12292
  (3 other events, 4.9 us)
Sparse Core Ops, SparseCore 0:
  373.4 35.1 all-gather.2
